TPU v7x, 256 devices: a whole 4x4x8 slice. The times are simulated.
256 devices in a mesh: col: 64 (over z, x, core), rhs: 4 (over y).
Axes of the slice: x: 4, y: 4, z: 8, core: 2. Of those that a mesh axis runs over, the one named last changes fastest.
Arguments:
- rhs_block: bfloat16 [16384, 4096], P('col', 'rhs'), may hold values from -6 to 6
- solution: bfloat16 [196608, 4096], P('col', 'rhs'), may hold values from -6 to 6
- factor: bfloat16 [64, 6, 256, 3072], P('col', None, 'rhs'), may hold values from -0.109375 to 0.109375
- tile_list: int32 [64, 6], P('col'), may hold values 0 or 1
- diag_inverse: bfloat16 [64, 256, 256], P('col'), may hold values from -0.375 to 0.375
Outputs:
- solved_rows: bfloat16 [16384, 4096], P('col', 'rhs')
All inputs are finite; a program needn't handle non-finite values. No bound on the sum of `tile_list` on one device may be relied on, other than what follows from the above.
Results may differ from a plain program's by a relative error of at most 0.0049.
Values may be sent and summed in bfloat16 or wider, within the bound.
A program may use at most 64 MiB of HBM per device.

v0:
```python
import jax
import jax.numpy as jnp
from jax import lax
from jax.sharding import PartitionSpec as P


def from_behind(block, axis, distance):
    devices = range(lax.axis_size(axis))
    route = [((i - distance) % len(devices), i) for i in devices]
    return lax.ppermute(block, axis, route)


def per_device(rhs_block, solution, factor, tile_list, diag_inverse):
    hop_count = factor.shape[1]
    carried = jnp.zeros((rhs_block.shape[0], rhs_block.shape[1]), jnp.float32)
    for offset in reversed(range(hop_count)):
        product_term = jnp.dot(
            lax.all_gather(factor[0, offset], "rhs", axis=0, tiled=True),
            solution,
            preferred_element_type=jnp.float32,
        )
        carried = carried + product_term * tile_list[0, offset].astype(jnp.float32)
        carried = from_behind(carried, "col", 1)
    remaining = (rhs_block.astype(jnp.float32) - carried).astype(jnp.bfloat16)
    return jnp.dot(diag_inverse[0], remaining, preferred_element_type=jnp.float32).astype(
        jnp.bfloat16
    )


def solution(mesh):
    in_specs = (
        P("col", "rhs"),
        P("col", "rhs"),
        P("col", None, "rhs", None),
        P("col", None),
        P("col", None, None),
    )
    out_specs = P("col", "rhs")
    return jax.shard_map(
        per_device, mesh=mesh, in_specs=in_specs, out_specs=out_specs, check_vma=False
    )
```

profile of v0, /device:TPU:1, one launch (start us, length us, event | category | flops | bytes accessed | tf_op | source)
XLA Modules:
  0.0 223.5 jit_solution(13746546917414927949)
XLA Ops:
  6.5 3.0 %fusion.35 = (bf16[1,1,64,3072]{3,2,1,0:T(8,128)(2,1)}, bf16[1,1,64,3072]{3,2,1,0:T(8,128)(2,1)}, bf16[1,1,64,3072]{3,2,1,0:T(8,128)(2,1)}, bf16[1,1,64,3072]{3,...) fusion(bf16[1,6,64,3072]{3,2,1,0:T(8,128)(2,1)} %param.7), kind=kLoop, calls=%fused_computation.23 | loop fusion | bytes 4718592 | tf_op jit(solution)/shard_map/slice | solution.py:18
  9.6 0.0 all-gather.15.cloned.1.call-start
  9.7 0.7 all-gather.15.cloned.1.call-update
  10.4 0.7 all-gather.17.cloned.1.call-update
  11.1 0.5 all-gather.19.cloned.1.call-update
  11.7 0.7 fusion.36
  13.0 29.4 %all-gather.13.cloned.1.call-done = bf16[1,1,256,3072]{3,2,1,0:T(8,128)(2,1)} async-done(((bf16[1,1,64,3072]{3,2,1,0:T(8,128)(2,1)}), bf16[1,1,256,3072]{3,2,1,0:T(8,128)(2,1)}) %all-gather.13.cloned.1.call-update) | async-done | bytes 1572880 | tf_op jit(solution)/shard_map/all_gather | solution.py:18
  42.4 5.1 %fusion.12 = f32[256,1024]{1,0:T(8,128)S(1)} fusion(bf16[3072,1024]{1,0:T(8,128)(2,1)} %param.6, bf16[1,1,256,3072]{3,2,1,0:T(8,128)(2,1)} %all-gather.13.cloned.1.call-done, f32[]{:T(128)} %bitcast.1), kind=kOutput, calls=%fused_computation.12 | convolution fusion | flops 1610874880 | bytes 8912900 | tf_op jit(solution)/shard_map/dot_general | solution.py:17
  47.5 2.0 collective-permute-start
  49.5 0.0 all-gather.23.cloned.1.call-start
  50.1 23.2 %all-gather.15.cloned.1.call-done = bf16[1,1,256,3072]{3,2,1,0:T(8,128)(2,1)} async-done(((bf16[1,1,64,3072]{3,2,1,0:T(8,128)(2,1)}), bf16[1,1,256,3072]{3,2,1,0:T(8,128)(2,1)}) %all-gather.15.cloned.1.call-update) | async-done | bytes 1572880 | tf_op jit(solution)/shard_map/all_gather | solution.py:18
  73.3 5.1 %fusion.30 = f32[256,1024]{1,0:T(8,128)S(1)} fusion(f32[256,1024]{1,0:T(8,128)S(1)} %collective-permute-done, bf16[3072,1024]{1,0:T(8,128)(2,1)} %param.6, bf16[1,1,256,3072]{3,2,1,0:T(8,128)(2,1)} %all-gather.15.cloned.1.call-done, f32[]{:T(128)} %bitcast.3), kind=kOutput, calls=%fused_computation.18 | convolution fusion | flops 1611137024 | bytes 9961476 | tf_op jit(solution)/shard_map/dot_general | solution.py:17
  78.4 2.0 collective-permute-start.1
  81.0 23.2 %all-gather.17.cloned.1.call-done = bf16[1,1,256,3072]{3,2,1,0:T(8,128)(2,1)} async-done(((bf16[1,1,64,3072]{3,2,1,0:T(8,128)(2,1)}), bf16[1,1,256,3072]{3,2,1,0:T(8,128)(2,1)}) %all-gather.17.cloned.1.call-update) | async-done | bytes 1572880 | tf_op jit(solution)/shard_map/all_gather | solution.py:18
  104.1 5.1 %fusion.18 = f32[256,1024]{1,0:T(8,128)S(1)} fusion(bf16[3072,1024]{1,0:T(8,128)(2,1)} %param.6, bf16[1,1,256,3072]{3,2,1,0:T(8,128)(2,1)} %all-gather.17.cloned.1.call-done, f32[]{:T(128)} %bitcast.5), kind=kOutput, calls=%fused_computation.14 | convolution fusion | flops 1610874880 | bytes 8912900 | tf_op jit(solution)/shard_map/dot_general | solution.py:17
  109.2 0.2 add.16
  109.4 2.0 collective-permute-start.2
  112.0 22.9 %all-gather.19.cloned.1.call-done = bf16[1,1,256,3072]{3,2,1,0:T(8,128)(2,1)} async-done(((bf16[1,1,64,3072]{3,2,1,0:T(8,128)(2,1)}), bf16[1,1,256,3072]{3,2,1,0:T(8,128)(2,1)}) %all-gather.19.cloned.1.call-update) | async-done | bytes 1572880 | tf_op jit(solution)/shard_map/all_gather | solution.py:18
  134.9 5.1 %fusion.21 = f32[256,1024]{1,0:T(8,128)S(1)} fusion(bf16[3072,1024]{1,0:T(8,128)(2,1)} %param.6, bf16[1,1,256,3072]{3,2,1,0:T(8,128)(2,1)} %all-gather.19.cloned.1.call-done, f32[]{:T(128)} %bitcast.7), kind=kOutput, calls=%fused_computation.15 | convolution fusion | flops 1610874880 | bytes 8912900 | tf_op jit(solution)/shard_map/dot_general | solution.py:17
  139.9 0.2 add.17
  140.1 2.0 collective-permute-start.3
  142.8 22.8 %all-gather.21.cloned.1.call-done = bf16[1,1,256,3072]{3,2,1,0:T(8,128)(2,1)} async-done(((bf16[1,1,64,3072]{3,2,1,0:T(8,128)(2,1)}), bf16[1,1,256,3072]{3,2,1,0:T(8,128)(2,1)}) %all-gather.21.cloned.1.call-update) | async-done | bytes 1572880 | tf_op jit(solution)/shard_map/all_gather | solution.py:18
  165.6 5.1 %fusion.24 = f32[256,1024]{1,0:T(8,128)S(1)} fusion(bf16[3072,1024]{1,0:T(8,128)(2,1)} %param.6, bf16[1,1,256,3072]{3,2,1,0:T(8,128)(2,1)} %all-gather.21.cloned.1.call-done, f32[]{:T(128)} %bitcast.9), kind=kOutput, calls=%fused_computation.16 | convolution fusion | flops 1610874880 | bytes 8912900 | tf_op jit(solution)/shard_map/dot_general | solution.py:17
  170.6 0.2 add.18
  170.8 2.2 collective-permute-start.4
  173.6 22.7 %all-gather.23.cloned.1.call-done = bf16[1,1,256,3072]{3,2,1,0:T(8,128)(2,1)} async-done(((bf16[1,1,64,3072]{3,2,1,0:T(8,128)(2,1)}), bf16[1,1,256,3072]{3,2,1,0:T(8,128)(2,1)}) %all-gather.23.cloned.1.call-update) | async-done | bytes 1572880 | tf_op jit(solution)/shard_map/all_gather | solution.py:18
  196.3 5.1 %fusion.27 = f32[256,1024]{1,0:T(8,128)S(1)} fusion(bf16[3072,1024]{1,0:T(8,128)(2,1)} %param.6, bf16[1,1,256,3072]{3,2,1,0:T(8,128)(2,1)} %all-gather.23.cloned.1.call-done, f32[]{:T(128)} %bitcast.11), kind=kOutput, calls=%fused_computation.17 | convolution fusion | flops 1610874880 | bytes 8912900 | tf_op jit(solution)/shard_map/dot_general | solution.py:17
  201.4 0.2 add.19
  201.5 2.0 collective-permute-start.5
  203.5 11.7 %collective-permute-done.5 = f32[256,1024]{1,0:T(8,128)S(1)} collective-permute-done((f32[256,1024]{1,0:T(8,128)S(1)}, f32[256,1024]{1,0:T(8,128)S(1)}, u32[]{:S(2)}, u32[]{:S(2)}) %collective-permute-start.5) | collective-permute-done | bytes 1048608 | tf_op jit(solution)/shard_map/ppermute | solution.py:10
  215.3 0.4 fusion.33
  215.7 1.0 copy.6
  (18 shorter events, 0.2 us)
Async XLA Ops:
  6.5 208.7 %copy-start = (bf16[1,256,256]{2,1,0:T(8,128)(2,1)S(1)}, bf16[1,256,256]{2,1,0:T(8,128)(2,1)}, u32[]{:S(2)}) copy-start(bf16[1,256,256]{2,1,0:T(8,128)(2,1)} %param.9) | copy-start | bytes 393220
  6.5 35.9 %all-gather.13.cloned.1.call-start = ((), (), s32[]{:S(2)}) async-start(), calls=%async_computation | async-start | bytes 1966080 | tf_op jit(solution)/shard_map/all_gather | solution.py:18
  9.6 2.1 copy-start.2
  9.6 63.7 %all-gather.15.cloned.1.call-start = ((), (), s32[]{:S(2)}) async-start(), calls=%async_computation.1 | async-start | bytes 1966080 | tf_op jit(solution)/shard_map/all_gather | solution.py:18
  10.4 93.8 %all-gather.17.cloned.1.call-start = ((), (), s32[]{:S(2)}) async-start(), calls=%async_computation.2 | async-start | bytes 1966080 | tf_op jit(solution)/shard_map/all_gather | solution.py:18
  11.1 123.8 %all-gather.19.cloned.1.call-start = ((), (), s32[]{:S(2)}) async-start(), calls=%async_computation.3 | async-start | bytes 1966080 | tf_op jit(solution)/shard_map/all_gather | solution.py:18
  11.7 153.9 %all-gather.21.cloned.1.call-start = ((), (), s32[]{:S(2)}) async-start(), calls=%async_computation.4 | async-start | bytes 1966080 | tf_op jit(solution)/shard_map/all_gather | solution.py:18
  47.5 25.8 %collective-permute-start = (f32[256,1024]{1,0:T(8,128)S(1)}, f32[256,1024]{1,0:T(8,128)S(1)}, u32[]{:S(2)}, u32[]{:S(2)}) collective-permute-start(f32[256,1024]{1,0:T(8,128)S(1)} %fusion.12), channel_id=1, source_target_pairs={{252,0},{0,4},{4,8},{8,12},{12,16},{16,20},{20,24},{24,28},{28,32}... | collective-permute-start | bytes 3145736 | tf_op jit(solution)/shard_map/ppermute | solution.py:10
  49.5 146.8 %all-gather.23.cloned.1.call-start = ((), (), s32[]{:S(2)}) async-start(), calls=%async_computation.5 | async-start | bytes 1966080 | tf_op jit(solution)/shard_map/all_gather | solution.py:18
  78.4 30.9 %collective-permute-start.1 = (f32[256,1024]{1,0:T(8,128)S(1)}, f32[256,1024]{1,0:T(8,128)S(1)}, u32[]{:S(2)}, u32[]{:S(2)}) collective-permute-start(f32[256,1024]{1,0:T(8,128)S(1)} %fusion.30), channel_id=1, source_target_pairs={{252,0},{0,4},{4,8},{8,12},{12,16},{16,20},{20,24},{24,28},{28,32}... | collective-permute-start | bytes 3145736 | tf_op jit(solution)/shard_map/ppermute | solution.py:10
  109.4 30.5 %collective-permute-start.2 = (f32[256,1024]{1,0:T(8,128)S(1)}, f32[256,1024]{1,0:T(8,128)S(1)}, u32[]{:S(2)}, u32[]{:S(2)}) collective-permute-start(f32[256,1024]{1,0:T(8,128)S(1)} %add.16), channel_id=1, source_target_pairs={{252,0},{0,4},{4,8},{8,12},{12,16},{16,20},{20,24},{24,28},{28,32}... | collective-permute-start | bytes 3145736 | tf_op jit(solution)/shard_map/ppermute | solution.py:10
  140.1 30.5 %collective-permute-start.3 = (f32[256,1024]{1,0:T(8,128)S(1)}, f32[256,1024]{1,0:T(8,128)S(1)}, u32[]{:S(2)}, u32[]{:S(2)}) collective-permute-start(f32[256,1024]{1,0:T(8,128)S(1)} %add.17), channel_id=1, source_target_pairs={{252,0},{0,4},{4,8},{8,12},{12,16},{16,20},{20,24},{24,28},{28,32}... | collective-permute-start | bytes 3145736 | tf_op jit(solution)/shard_map/ppermute | solution.py:10
  170.8 30.6 %collective-permute-start.4 = (f32[256,1024]{1,0:T(8,128)S(1)}, f32[256,1024]{1,0:T(8,128)S(1)}, u32[]{:S(2)}, u32[]{:S(2)}) collective-permute-start(f32[256,1024]{1,0:T(8,128)S(1)} %add.18), channel_id=1, source_target_pairs={{252,0},{0,4},{4,8},{8,12},{12,16},{16,20},{20,24},{24,28},{28,32}... | collective-permute-start | bytes 3145736 | tf_op jit(solution)/shard_map/ppermute | solution.py:10
  201.3 13.9 %copy-start.1 = (bf16[256,1024]{1,0:T(8,128)(2,1)S(1)}, bf16[256,1024]{1,0:T(8,128)(2,1)}, u32[]{:S(2)}) copy-start(bf16[256,1024]{1,0:T(8,128)(2,1)} %param.5) | copy-start | bytes 1572868
  201.5 13.7 %collective-permute-start.5 = (f32[256,1024]{1,0:T(8,128)S(1)}, f32[256,1024]{1,0:T(8,128)S(1)}, u32[]{:S(2)}, u32[]{:S(2)}) collective-permute-start(f32[256,1024]{1,0:T(8,128)S(1)} %add.19), channel_id=1, source_target_pairs={{252,0},{0,4},{4,8},{8,12},{12,16},{16,20},{20,24},{24,28},{28,32}... | collective-permute-start | bytes 3145736 | tf_op jit(solution)/shard_map/ppermute | solution.py:10
Sparse Core Ops, SparseCore 0:
  9.7 32.6 all-gather.12
  44.2 29.0 all-gather.14
  75.1 29.0 all-gather.16
  105.8 29.0 all-gather.18
  136.5 29.0 all-gather.20
  167.2 29.0 all-gather.22
where the time goes:
time: 226 us; the launch traced here: 224 us
  waiting for transfers between devices  158 us (70%)
  matrix products  30.8 us (14%)
  between operations  17.3 us (8%)
  starting transfers between devices  12.3 us (5%)
  local copies, waits for them, and re-layouts  4.73 us (2%)
    all_gather x6, waiting for transfers between devices, per_device(): lax.all_gather(factor[0, offset], 'rhs', axis=0, tiled=True)  144 us
    dot_general x6, matrix products, per_device(): jnp.dot(lax.all_gather(factor[0, offset], 'rhs', axis=0, tiled=True), sol...  30.4 us
    ppermute x6, starting transfers between devices, from_behind(): return lax.ppermute(block, axis, route)  12.1 us
    ppermute x6, waiting for transfers between devices, from_behind(): return lax.ppermute(block, axis, route)  11.8 us
  transfers between devices with their start and end apart: 12, of which 7 were waited for; matrix products, arithmetic and copies ran while one was open for 14% of the time, Pallas kernels for 0%

commit v1 on v0

v1 whole, which is shorter than its diff:
```python
import functools

import jax
import jax.numpy as jnp
from jax import lax
from jax.experimental import pallas as pl
from jax.experimental.pallas import tpu as pltpu
from jax.sharding import PartitionSpec as P

MESH = pl.DeviceIdType.MESH


def kernel(n_col, n_rhs, order, tiles_ref, rhs_hbm, sol_hbm, fac_hbm, dia_hbm, out_ref,
           sol, fac, rhs, dia, acc, rem, part, got,
           load_sem, y_send, y_recv, x_send, x_recv):
    hops, quarter = fac_hbm.shape[1], fac_hbm.shape[2]
    rows, cols = rhs_hbm.shape
    half = quarter // 2
    wide = min(256, cols)
    col, row = lax.axis_index("col"), lax.axis_index("rhs")
    up, down = lax.rem(row + 1, n_rhs), lax.rem(row + n_rhs - 1, n_rhs)

    loads = [
        pltpu.make_async_copy(fac_hbm.at[0], fac.at[:, pl.ds(0, quarter), :], load_sem.at[0]),
        pltpu.make_async_copy(sol_hbm, sol, load_sem.at[1]),
        pltpu.make_async_copy(rhs_hbm, rhs, load_sem.at[2]),
        pltpu.make_async_copy(dia_hbm.at[0], dia, load_sem.at[3]),
    ]
    for load in loads:
        load.start()

    barrier = pltpu.get_barrier_semaphore()
    for peer in (up, down):
        pl.semaphore_signal(barrier, inc=1, device_id=(col, peer), device_id_type=MESH)
    for hop in range(1, hops + 1):
        for peer in (lax.rem(col + hop, n_col), lax.rem(col + n_col - hop, n_col)):
            pl.semaphore_signal(barrier, inc=1, device_id=(peer, row), device_id_type=MESH)
    pl.semaphore_wait(barrier, 2 + 2 * hops)

    def y_copy(src, tile, start, size, kind, peer):
        return pltpu.make_async_remote_copy(
            src_ref=src,
            dst_ref=fac.at[tile, pl.ds(start, size), :],
            send_sem=y_send.at[tile, kind],
            recv_sem=y_recv.at[tile, kind],
            device_id=(col, peer),
            device_id_type=MESH,
        )

    def own(tile):
        return (
            y_copy(fac_hbm.at[0, tile], tile, quarter, quarter, 0, up),
            y_copy(fac_hbm.at[0, tile], tile, 2 * quarter, quarter, 1, down),
        )

    def relay(tile):
        return (
            y_copy(fac.at[tile, pl.ds(quarter, half), :], tile, 3 * quarter, half, 2, up),
            y_copy(fac.at[tile, pl.ds(2 * quarter + half, half), :], tile, 3 * quarter + half, half, 3, down),
        )

    def product(tile, start, size):
        weight = tiles_ref[0, tile].astype(jnp.float32)

        @pl.loop(0, cols // wide)
        def _(block):
            at = pl.ds(pl.multiple_of(block * wide, wide), wide)
            term = jnp.dot(
                fac[tile, pl.ds(start, size), :], sol[:, at], preferred_element_type=jnp.float32
            )
            part[tile, pl.ds(start, size), at] = (term * weight).astype(jnp.bfloat16)

    def send(tile, start, size, kind):
        return pltpu.make_async_remote_copy(
            src_ref=part.at[tile, pl.ds(start, size), :],
            dst_ref=got.at[tile, pl.ds(start, size), :],
            send_sem=x_send.at[kind],
            recv_sem=x_recv.at[kind],
            device_id=(lax.rem(col + tile + 1, n_col), row),
            device_id_type=MESH,
        )

    def add(tile, start, size, first=False):
        at = pl.ds(start, size)
        term = got[tile, at, :].astype(jnp.float32)
        acc[at, :] = term if first else acc[at, :] + term

    sends = []

    def go(copy):
        copy.start()
        sends.append(copy)

    for tile in order[:2]:
        for copy in own(tile):
            go(copy)
    loads[0].wait()
    loads[1].wait()

    arrivals = []
    for step, tile in enumerate(order):
        for copy, onward in zip(own(tile), relay(tile)):
            copy.wait_recv()
            go(onward)
        if step + 2 < hops:
            for copy in own(order[step + 2]):
                go(copy)
        if step >= 1:
            before = order[step - 1]
            for copy in relay(before):
                copy.wait_recv()
            product(before, 0, rows)
            out = send(before, 0, rows, before)
            go(out)
            arrivals.append((before, out))
        if step >= 3:
            done, arrival = arrivals.pop(0)
            arrival.wait_recv()
            add(done, 0, rows, first=step == 3)
    last = order[-1]
    product(last, 0, 3 * quarter)
    early = send(last, 0, 3 * quarter, last)
    go(early)
    for copy in relay(last):
        copy.wait_recv()
    product(last, 3 * quarter, quarter)
    late = send(last, 3 * quarter, quarter, hops)
    go(late)
    loads[2].wait()
    loads[3].wait()
    for done, arrival in arrivals:
        arrival.wait_recv()
        add(done, 0, rows)
    for arrival, start, size in ((early, 0, 3 * quarter), (late, 3 * quarter, quarter)):
        arrival.wait_recv()
        add(last, start, size)
    for slot, peer in enumerate((row, down, up, lax.rem(row + 2, n_rhs))):
        at = pl.ds(pl.multiple_of(peer * quarter, quarter), quarter)
        rem[at, :] = (
            rhs[at, :].astype(jnp.float32) - acc[pl.ds(slot * quarter, quarter), :]
        ).astype(jnp.bfloat16)
    out_ref[...] = jnp.dot(dia[...], rem[...], preferred_element_type=jnp.float32).astype(jnp.bfloat16)
    for copy in sends:
        copy.wait_send()


ORDER = (3, 4, 2, 5, 1, 0)


def per_device(rhs_block, sol, factor, tile_list, diag_inverse):
    n_col, n_rhs = lax.axis_size("col"), lax.axis_size("rhs")
    rows, cols = rhs_block.shape
    depth = sol.shape[0]
    hops = factor.shape[1]
    any_space = pl.BlockSpec(memory_space=pl.ANY)
    return pl.pallas_call(
        functools.partial(kernel, n_col, n_rhs, ORDER),
        out_shape=jax.ShapeDtypeStruct((rows, cols), jnp.bfloat16),
        in_specs=[pl.BlockSpec(memory_space=pltpu.SMEM)] + [any_space] * 4,
        out_specs=pl.BlockSpec(memory_space=pltpu.VMEM),
        scratch_shapes=[
            pltpu.VMEM((depth, cols), jnp.bfloat16),
            pltpu.VMEM((hops, rows, depth), jnp.bfloat16),
            pltpu.VMEM((rows, cols), jnp.bfloat16),
            pltpu.VMEM((rows, rows), jnp.bfloat16),
            pltpu.VMEM((rows, cols), jnp.float32),
            pltpu.VMEM((rows, cols), jnp.bfloat16),
            pltpu.VMEM((hops, rows, cols), jnp.bfloat16),
            pltpu.VMEM((hops, rows, cols), jnp.bfloat16),
            pltpu.SemaphoreType.DMA((4,)),
            pltpu.SemaphoreType.DMA((hops, 4)),
            pltpu.SemaphoreType.DMA((hops, 4)),
            pltpu.SemaphoreType.DMA((hops + 1,)),
            pltpu.SemaphoreType.DMA((hops + 1,)),
        ],
        compiler_params=pltpu.CompilerParams(
            collective_id=0, has_side_effects=True, vmem_limit_bytes=60 * 1024 * 1024
        ),
    )(tile_list, rhs_block, sol, factor, diag_inverse)


def solution(mesh):
    in_specs = (
        P("col", "rhs"),
        P("col", "rhs"),
        P("col", None, "rhs", None),
        P("col", None),
        P("col", None, None),
    )
    return jax.shard_map(
        per_device, mesh=mesh, in_specs=in_specs, out_specs=P("col", "rhs"), check_vma=False
    )
```

time: 226 us -> 109 us (0.48)
  waiting for transfers between devices: 158 us -> 0 us
  Pallas kernels: 0 us -> 107 us
  matrix products: 30.8 us -> 0 us
  between operations: 17.3 us -> 0.01 us
  starting transfers between devices: 12.3 us -> 0 us
  local copies, waits for them, and re-layouts: 4.73 us -> 1.87 us
    all_gather x6 -> x0, waiting for transfers between devices: 144 us -> none  [per_device(): lax.all_gather(factor[0, offset], 'rhs', axis=0, tiled=True)]
    pallas_call x0 -> x1, Pallas kernels: none -> 107 us  [per_device(): pl.pallas_call(functools.partial(kernel, n_col, n_rhs, ORDER), out_shape=...]
    dot_general x7 -> x0, matrix products: 30.8 us -> none  [the longest x6 30.4 us: per_device(): jnp.dot(lax.all_gather(factor[0, offset], 'rhs', axis=0, tiled=True), sol...]
    ppermute x6 -> x0, starting transfers between devices: 12.1 us -> none  [from_behind(): return lax.ppermute(block, axis, route)]
    ppermute x6 -> x0, waiting for transfers between devices: 11.8 us -> none  [from_behind(): return lax.ppermute(block, axis, route)]
    slice x2 -> x0, local copies, waits for them, and re-layouts: 3.71 us -> none  [the longest x1 3.04 us: per_device(): factor[0, offset]]
  transfers between devices with their start and end apart: 12 -> 0, of which waited for: 7 -> 0; matrix products, arithmetic and copies ran while one was open for 14% -> 0% of each run, Pallas kernels for 0% -> 0%
where the time goes in v1:
time: 109 us; the launch traced here: 108 us
  Pallas kernels  107 us (98%)
  local copies, waits for them, and re-layouts  1.87 us (2%)
    pallas_call x1, Pallas kernels, per_device(): pl.pallas_call(functools.partial(kernel, n_col, n_rhs, ORDER), out_shape=...  107 us

profile of v1, /device:TPU:1, one launch (start us, length us, event | category | flops | bytes accessed | tf_op | source)
XLA Modules:
  0.0 108.5 jit_solution(16800957476677654531)
XLA Ops:
  0.0 106.6 %shard_map.55 = bf16[256,1024]{1,0:T(8,128)(2,1)} custom-call(s32[1,6]{1,0:T(1,128)} %tiles_ref.1, bf16[256,1024]{1,0:T(8,128)(2,1)} %rhs_hbm.1, bf16[3072,1024]{1,0:T(8,128)(2,1)} %sol_hbm.1, bf16[1,6,64,3072]{3,2,1,0:T(8,128)(2,1)} %fac_hbm.1, bf16[1,256,256]{2,1,0:T(8,128)(2,1)} %dia_hbm.1), custom_call_target="tpu_custom_call" | custom-call | tf_op jit(solution)/shard_map/pallas_call | solution.py:156
  106.6 1.9 %copy.7 = bf16[256,1024]{1,0:T(8,128)(2,1)} copy(bf16[256,1024]{1,0:T(8,128)(2,1)} %shard_map.55) | data formatting | bytes 1048576

commit v2 on v0

v2 whole, which is shorter than its diff:
```python
import functools

import jax
import jax.numpy as jnp
from jax import lax
from jax.experimental import pallas as pl
from jax.experimental.pallas import tpu as pltpu
from jax.sharding import PartitionSpec as P

MESH = pl.DeviceIdType.MESH
PAIRED = (4, 5, 6, 3, 2)
PIECES = 4


def kernel(n_col, n_rhs, tiles_ref, rhs_hbm, sol_hbm, fac_hbm, dia_hbm, out_ref,
           sol, fac, rhs, dia, acc, rem, keep, give, take, part, got, tail, near, last,
           load_sem, y_send, y_recv, z_send, z_recv, c_send, c_recv, x_send, x_recv, t_send, t_recv, turn):
    hops, quarter = fac_hbm.shape[1], fac_hbm.shape[2]
    depth = fac_hbm.shape[3]
    rows, cols = rhs_hbm.shape
    half = quarter // 2
    side = cols // 2
    wide = min(256, side)
    piece = depth // PIECES
    most = rows - quarter
    pairs = len(PAIRED)
    col, row = lax.axis_index("col"), lax.axis_index("rhs")
    core = lax.rem(col, 2)
    base = col - core
    partner = base + 1 - core
    up, down = lax.rem(row + 1, n_rhs), lax.rem(row + n_rhs - 1, n_rhs)
    tile_of = [ahead - 1 - core for ahead in PAIRED] + [(hops - 1) * core]

    loads = [
        pltpu.make_async_copy(fac_hbm.at[0, tile_of[s]], fac.at[s, pl.ds(0, quarter), :], load_sem.at[s])
        for s in range(hops)
    ]
    loads += [
        pltpu.make_async_copy(sol_hbm, sol, load_sem.at[hops]),
        pltpu.make_async_copy(rhs_hbm, rhs, load_sem.at[hops + 1]),
        pltpu.make_async_copy(dia_hbm.at[0], dia, load_sem.at[hops + 2]),
    ]

    barrier = pltpu.get_barrier_semaphore()
    for peer in (up, down):
        pl.semaphore_signal(barrier, inc=1, device_id=(col, peer), device_id_type=MESH)
    pl.semaphore_signal(barrier, inc=1, device_id=(partner, row), device_id_type=MESH)
    for back in (2, 4, 6):
        for which in (0, 1):
            source = lax.rem(base + n_col - back + which, n_col)
            pl.semaphore_signal(barrier, inc=1, device_id=(source, row), device_id_type=MESH)
    for load in loads:
        load.start()
    pl.semaphore_wait(barrier, 9)

    def remote(src, dst, send, recv, device):
        return pltpu.make_async_remote_copy(
            src_ref=src, dst_ref=dst, send_sem=send, recv_sem=recv, device_id=device, device_id_type=MESH
        )

    def y_copy(src, s, start, size, kind, peer):
        return remote(
            src, fac.at[s, pl.ds(start, size), :], y_send.at[s, kind], y_recv.at[s, kind], (col, peer)
        )

    def own(s):
        src = fac_hbm.at[0, tile_of[s]]
        return (
            y_copy(src, s, quarter, quarter, 0, up),
            y_copy(src, s, 2 * quarter, quarter, 1, down),
        )

    def relay(s):
        return (
            y_copy(fac.at[s, pl.ds(quarter, half), :], s, 3 * quarter, half, 2, up),
            y_copy(fac.at[s, pl.ds(2 * quarter + half, half), :], s, 3 * quarter + half, half, 3, down),
        )

    final = hops - 1

    def z_copy(src, p, start, size, kind, peer):
        at = pl.ds(p * piece, piece)
        return remote(
            src.at[:, at], fac.at[final, pl.ds(start, size), at], z_send.at[p, kind], z_recv.at[p, kind], (col, peer)
        )

    def own_piece(p):
        src = fac_hbm.at[0, tile_of[final]]
        return (
            z_copy(src, p, quarter, quarter, 0, up),
            z_copy(src, p, 2 * quarter, quarter, 1, down),
        )

    def relay_piece(p):
        return (
            z_copy(fac.at[final, pl.ds(quarter, half), :], p, 3 * quarter, half, 2, up),
            z_copy(fac.at[final, pl.ds(2 * quarter + half, half), :], p, 3 * quarter + half, half, 3, down),
        )

    def weight(s):
        return tiles_ref[0, tile_of[s]].astype(jnp.float32)

    def product(s):
        scale = weight(s)
        for target, which in ((give, 1 - core), (keep, core)):

            @pl.loop(0, side // wide)
            def _(block):
                at = pl.multiple_of(which * side + block * wide, wide)
                term = jnp.dot(fac[s], sol[:, pl.ds(at, wide)], preferred_element_type=jnp.float32)
                target[s, :, pl.ds(pl.multiple_of(block * wide, wide), wide)] = term * scale

            if target is give:
                swap(s).start()

    def swap(s):
        return remote(give.at[s], take.at[s], c_send.at[s], c_recv.at[s], (partner, row))

    def onward(s):
        ahead = PAIRED[s]
        slot = ahead // 2 - 1
        return remote(
            part.at[s], got.at[slot, core], x_send.at[s], x_recv.at[slot, core],
            (lax.rem(base + ahead, n_col), row),
        )

    def combine(s):
        swap(s).wait_recv()
        part[s] = (keep[s] + take[s]).astype(jnp.bfloat16)
        onward(s).start()

    def arrived(slot, which):
        return remote(part.at[0], got.at[slot, which], x_send.at[0], x_recv.at[slot, which], (partner, row))

    def add(slot, first=False):
        for which in (0, 1):
            arrived(slot, which).wait_recv()
            at = pl.ds(which * side, side)
            term = got[slot, which].astype(jnp.float32)
            acc[:, at] = term if first else acc[:, at] + term

    def close(start, size, kind):
        at = pl.ds(start, size)
        inside = remote(tail.at[at, :], near.at[at, :], t_send.at[kind], t_recv.at[0, kind], (partner, row))
        outside = remote(
            last.at[:, at, :], got.at[2, :, at, :], t_send.at[kind], t_recv.at[1, kind],
            (lax.rem(base + 7, n_col), row),
        )
        return inside, outside

    def product_most():
        scale = weight(final)

        @pl.loop(0, cols // wide)
        def _(block):
            at = pl.ds(pl.multiple_of(block * wide, wide), wide)
            term = jnp.dot(
                fac[final, pl.ds(0, most), :], sol[:, at], preferred_element_type=jnp.float32
            )
            tail[pl.ds(0, most), at] = term * scale

    def hand_over(start, size, kind):
        inside, outside = close(start, size, kind)

        @pl.when(core == 0)
        def _():
            inside.start()

        @pl.when(core == 1)
        def _():
            at = pl.ds(start, size)
            for which in (0, 1):
                last[which, at, :] = tail[at, pl.ds(which * side, side)].astype(jnp.bfloat16)
            outside.start()

    for s in (0, 1):
        for copy in own(s):
            copy.start()
    for load in loads:
        load.wait()

    for s in range(pairs):
        for copy, forward in zip(own(s), relay(s)):
            copy.wait_recv()
            forward.start()
        if s + 2 < pairs:
            for copy in own(s + 2):
                copy.start()
        elif s + 2 == pairs:

            @pl.when(core == 1)
            def _():
                for p in range(PIECES):
                    for copy in own_piece(p):
                        copy.start()

        if s >= 1:
            for copy in relay(s - 1):
                copy.wait_recv()
            product(s - 1)
        if s >= 2:
            combine(s - 2)
        if s == 4:
            add(1, first=True)

    def pass_on():
        for p in range(PIECES):
            for copy, forward in zip(own_piece(p), relay_piece(p)):
                copy.wait_recv()
                forward.start()

    @pl.when(core == 1)
    def _():
        pass_on()
        pl.semaphore_signal(turn, inc=1, device_id=(partner, row), device_id_type=MESH)
        product_most()

    for copy in relay(pairs - 1):
        copy.wait_recv()
    product(pairs - 1)

    @pl.when(core == 0)
    def _():
        pl.semaphore_wait(turn, 1)
        for p in range(PIECES):
            for copy in own_piece(p):
                copy.start()

    combine(pairs - 2)
    combine(pairs - 1)

    @pl.when(core == 0)
    def _():
        pass_on()
        product_most()

    hand_over(0, most, 0)
    for p in range(PIECES):
        for copy in relay_piece(p):
            copy.wait_recv()
        deep = pl.ds(p * piece, piece)

        @pl.loop(0, cols // wide)
        def _(block):
            at = pl.ds(pl.multiple_of(block * wide, wide), wide)
            term = jnp.dot(
                fac[final, pl.ds(most, quarter), deep], sol[deep, at], preferred_element_type=jnp.float32
            )
            if p > 0:
                term = term + tail[pl.ds(most, quarter), at]
            if p == PIECES - 1:
                term = term * weight(final)
            tail[pl.ds(most, quarter), at] = term

    hand_over(most, quarter, 1)
    add(0)

    @pl.when(core == 0)
    def _():
        add(2)

    @pl.when(core == 1)
    def _():
        for kind, start, size in ((0, 0, most), (1, most, quarter)):
            at = pl.ds(start, size)
            inside, outside = close(start, size, kind)
            outside.wait_recv()
            for which in (0, 1):
                there = pl.ds(which * side, side)
                acc[at, there] = acc[at, there] + got[2, which, at, :].astype(jnp.float32)
            inside.wait_recv()
            acc[at, :] = acc[at, :] + near[at, :]

    for slot, peer in enumerate((row, down, up, lax.rem(row + 2, n_rhs))):
        at = pl.ds(pl.multiple_of(peer * quarter, quarter), quarter)
        rem[at, :] = (
            rhs[at, :].astype(jnp.float32) - acc[pl.ds(slot * quarter, quarter), :]
        ).astype(jnp.bfloat16)
    out_ref[...] = jnp.dot(dia[...], rem[...], preferred_element_type=jnp.float32).astype(jnp.bfloat16)

    for s in range(pairs):
        for copy in own(s) + relay(s) + (swap(s), onward(s)):
            copy.wait_send()
    for p in range(PIECES):
        for copy in own_piece(p) + relay_piece(p):
            copy.wait_send()
    for kind, start, size in ((0, 0, most), (1, most, quarter)):
        inside, outside = close(start, size, kind)

        @pl.when(core == 0)
        def _():
            inside.wait_send()

        @pl.when(core == 1)
        def _():
            outside.wait_send()


def per_device(rhs_block, sol, factor, tile_list, diag_inverse):
    n_col, n_rhs = lax.axis_size("col"), lax.axis_size("rhs")
    rows, cols = rhs_block.shape
    depth = sol.shape[0]
    hops = factor.shape[1]
    pairs, side = len(PAIRED), cols // 2
    any_space = pl.BlockSpec(memory_space=pl.ANY)
    dma = pltpu.SemaphoreType.DMA
    return pl.pallas_call(
        functools.partial(kernel, n_col, n_rhs),
        out_shape=jax.ShapeDtypeStruct((rows, cols), jnp.bfloat16),
        in_specs=[pl.BlockSpec(memory_space=pltpu.SMEM)] + [any_space] * 4,
        out_specs=pl.BlockSpec(memory_space=pltpu.VMEM),
        scratch_shapes=[
            pltpu.VMEM((depth, cols), jnp.bfloat16),
            pltpu.VMEM((hops, rows, depth), jnp.bfloat16),
            pltpu.VMEM((rows, cols), jnp.bfloat16),
            pltpu.VMEM((rows, rows), jnp.bfloat16),
            pltpu.VMEM((rows, cols), jnp.float32),
            pltpu.VMEM((rows, cols), jnp.bfloat16),
            pltpu.VMEM((pairs, rows, side), jnp.float32),
            pltpu.VMEM((pairs, rows, side), jnp.float32),
            pltpu.VMEM((pairs, rows, side), jnp.float32),
            pltpu.VMEM((pairs, rows, side), jnp.bfloat16),
            pltpu.VMEM((3, 2, rows, side), jnp.bfloat16),
            pltpu.VMEM((rows, cols), jnp.float32),
            pltpu.VMEM((rows, cols), jnp.float32),
            pltpu.VMEM((2, rows, side), jnp.bfloat16),
            dma((hops + 3,)),
            dma((pairs, 4)),
            dma((pairs, 4)),
            dma((PIECES, 4)),
            dma((PIECES, 4)),
            dma((pairs,)),
            dma((pairs,)),
            dma((pairs,)),
            dma((3, 2)),
            dma((2,)),
            dma((2, 2)),
            pltpu.SemaphoreType.REGULAR,
        ],
        compiler_params=pltpu.CompilerParams(
            collective_id=0, has_side_effects=True, vmem_limit_bytes=60 * 1024 * 1024
        ),
    )(tile_list, rhs_block, sol, factor, diag_inverse)


def solution(mesh):
    in_specs = (
        P("col", "rhs"),
        P("col", "rhs"),
        P("col", None, "rhs", None),
        P("col", None),
        P("col", None, None),
    )
    return jax.shard_map(
        per_device, mesh=mesh, in_specs=in_specs, out_specs=P("col", "rhs"), check_vma=False
    )
```

time: 226 us -> 101 us (0.45)
  the two profiles are of different devices: /device:TPU:1 before, /device:TPU:5 now
where the time goes in v2:
time: 101 us
  Pallas kernels  99.1 us (98%)
  local copies, waits for them, and re-layouts  1.87 us (2%)
    pallas_call x1, Pallas kernels, per_device(): pl.pallas_call(functools.partial(kernel, n_col, n_rhs), out_shape=jax.Sha...  99.1 us

profile of v2, /device:TPU:5, one launch (start us, length us, event | category | flops | bytes accessed | tf_op | source)
XLA Modules:
  0.0 100.9 jit_solution(7924154043228592393)
XLA Ops:
  0.0 99.1 %shard_map.55 = bf16[256,1024]{1,0:T(8,128)(2,1)} custom-call(s32[1,6]{1,0:T(1,128)} %tiles_ref.1, bf16[256,1024]{1,0:T(8,128)(2,1)} %rhs_hbm.1, bf16[3072,1024]{1,0:T(8,128)(2,1)} %sol_hbm.1, bf16[1,6,64,3072]{3,2,1,0:T(8,128)(2,1)} %fac_hbm.1, bf16[1,256,256]{2,1,0:T(8,128)(2,1)} %dia_hbm.1), custom_call_target="tpu_custom_call" | custom-call | tf_op jit(solution)/shard_map/pallas_call | solution.py:307
  99.1 1.9 %copy.7 = bf16[256,1024]{1,0:T(8,128)(2,1)} copy(bf16[256,1024]{1,0:T(8,128)(2,1)} %shard_map.55) | data formatting | bytes 1048576

commit v3 on v2

--- a/solution.py
+++ b/solution.py
@@ -100,44 +100,55 @@
     def weight(s):
         return tiles_ref[0, tile_of[s]].astype(jnp.float32)
 
-    def product(s):
+    early, late = (0, most, 0), (most, quarter, 1)
+
+    def product(s, span):
         scale = weight(s)
+        lines = pl.ds(span[0], span[1])
         for target, which in ((give, 1 - core), (keep, core)):
 
             @pl.loop(0, side // wide)
             def _(block):
                 at = pl.multiple_of(which * side + block * wide, wide)
-                term = jnp.dot(fac[s], sol[:, pl.ds(at, wide)], preferred_element_type=jnp.float32)
-                target[s, :, pl.ds(pl.multiple_of(block * wide, wide), wide)] = term * scale
+                term = jnp.dot(fac[s, lines, :], sol[:, pl.ds(at, wide)], preferred_element_type=jnp.float32)
+                target[s, lines, pl.ds(pl.multiple_of(block * wide, wide), wide)] = term * scale
 
             if target is give:
-                swap(s).start()
-
-    def swap(s):
-        return remote(give.at[s], take.at[s], c_send.at[s], c_recv.at[s], (partner, row))
-
-    def onward(s):
-        ahead = PAIRED[s]
-        slot = ahead // 2 - 1
+                swap(s, span).start()
+
+    def swap(s, span):
+        start, size, kind = span
+        at = pl.ds(start, size)
         return remote(
-            part.at[s], got.at[slot, core], x_send.at[s], x_recv.at[slot, core],
-            (lax.rem(base + ahead, n_col), row),
-        )
-
-    def combine(s):
-        swap(s).wait_recv()
-        part[s] = (keep[s] + take[s]).astype(jnp.bfloat16)
-        onward(s).start()
-
-    def arrived(slot, which):
-        return remote(part.at[0], got.at[slot, which], x_send.at[0], x_recv.at[slot, which], (partner, row))
-
-    def add(slot, first=False):
+            give.at[s, at, :], take.at[s, at, :], c_send.at[s, kind], c_recv.at[s, kind], (partner, row)
+        )
+
+    def onward(s, span):
+        start, size, kind = span
+        at = pl.ds(start, size)
+        slot = PAIRED[s] // 2 - 1
+        return remote(
+            part.at[s, at, :], got.at[slot, core, at, :], x_send.at[s, kind], x_recv.at[slot, kind, core],
+            (lax.rem(base + PAIRED[s], n_col), row),
+        )
+
+    def combine(s, span):
+        at = pl.ds(span[0], span[1])
+        swap(s, span).wait_recv()
+        part[s, at, :] = (keep[s, at, :] + take[s, at, :]).astype(jnp.bfloat16)
+        onward(s, span).start()
+
+    def add(slot, span, first=False):
+        start, size, kind = span
+        at = pl.ds(start, size)
         for which in (0, 1):
-            arrived(slot, which).wait_recv()
-            at = pl.ds(which * side, side)
-            term = got[slot, which].astype(jnp.float32)
-            acc[:, at] = term if first else acc[:, at] + term
+            remote(
+                part.at[0, at, :], got.at[slot, which, at, :], x_send.at[0, 0], x_recv.at[slot, kind, which],
+                (partner, row),
+            ).wait_recv()
+            there = pl.ds(which * side, side)
+            term = got[slot, which, at, :].astype(jnp.float32)
+            acc[at, there] = term if first else acc[at, there] + term
 
     def close(start, size, kind):
         at = pl.ds(start, size)
@@ -148,16 +159,18 @@
         )
         return inside, outside
 
-    def product_most():
-        scale = weight(final)
+    def partial(p, span):
+        lines, deep = pl.ds(span[0], span[1]), pl.ds(p * piece, piece)
 
         @pl.loop(0, cols // wide)
         def _(block):
             at = pl.ds(pl.multiple_of(block * wide, wide), wide)
-            term = jnp.dot(
-                fac[final, pl.ds(0, most), :], sol[:, at], preferred_element_type=jnp.float32
-            )
-            tail[pl.ds(0, most), at] = term * scale
+            term = jnp.dot(fac[final, lines, deep], sol[deep, at], preferred_element_type=jnp.float32)
+            if p > 0:
+                term = term + tail[lines, at]
+            if p == PIECES - 1:
+                term = term * weight(final)
+            tail[lines, at] = term
 
     def hand_over(start, size, kind):
         inside, outside = close(start, size, kind)
@@ -179,6 +192,7 @@
     for load in loads:
         load.wait()
 
+    end = pairs - 1
     for s in range(pairs):
         for copy, forward in zip(own(s), relay(s)):
             copy.wait_recv()
@@ -186,7 +200,7 @@
         if s + 2 < pairs:
             for copy in own(s + 2):
                 copy.start()
-        elif s + 2 == pairs:
+        if s == end:
 
             @pl.when(core == 1)
             def _():
@@ -194,30 +208,19 @@
                     for copy in own_piece(p):
                         copy.start()
 
+        product(s, early)
+        combine(s, early)
         if s >= 1:
             for copy in relay(s - 1):
                 copy.wait_recv()
-            product(s - 1)
-        if s >= 2:
-            combine(s - 2)
-        if s == 4:
-            add(1, first=True)
-
-    def pass_on():
-        for p in range(PIECES):
-            for copy, forward in zip(own_piece(p), relay_piece(p)):
-                copy.wait_recv()
-                forward.start()
-
-    @pl.when(core == 1)
-    def _():
-        pass_on()
-        pl.semaphore_signal(turn, inc=1, device_id=(partner, row), device_id_type=MESH)
-        product_most()
-
-    for copy in relay(pairs - 1):
+            product(s - 1, late)
+            combine(s - 1, late)
+    for span in (early, late):
+        add(1, span, first=True)
+    for copy in relay(end):
         copy.wait_recv()
-    product(pairs - 1)
+    product(end, late)
+    combine(end, late)
 
     @pl.when(core == 0)
     def _():
@@ -225,43 +228,37 @@
         for p in range(PIECES):
             for copy in own_piece(p):
                 copy.start()
-
-    combine(pairs - 2)
-    combine(pairs - 1)
-
-    @pl.when(core == 0)
-    def _():
-        pass_on()
-        product_most()
-
-    hand_over(0, most, 0)
+        for span in (early, late):
+            add(2, span)
+
+    for p in range(PIECES):
+        if p == PIECES - 1:
+
+            @pl.when(core == 1)
+            def _():
+                pl.semaphore_signal(turn, inc=1, device_id=(partner, row), device_id_type=MESH)
+
+        for copy, forward in zip(own_piece(p), relay_piece(p)):
+            copy.wait_recv()
+            forward.start()
+        partial(p, early)
+    hand_over(*early)
     for p in range(PIECES):
         for copy in relay_piece(p):
             copy.wait_recv()
-        deep = pl.ds(p * piece, piece)
-
-        @pl.loop(0, cols // wide)
-        def _(block):
-            at = pl.ds(pl.multiple_of(block * wide, wide), wide)
-            term = jnp.dot(
-                fac[final, pl.ds(most, quarter), deep], sol[deep, at], preferred_element_type=jnp.float32
-            )
-            if p > 0:
-                term = term + tail[pl.ds(most, quarter), at]
-            if p == PIECES - 1:
-                term = term * weight(final)
-            tail[pl.ds(most, quarter), at] = term
-
-    hand_over(most, quarter, 1)
-    add(0)
+        partial(p, late)
+    hand_over(*late)
 
     @pl.when(core == 0)
     def _():
-        add(2)
+        for span in (early, late):
+            add(0, span)
 
     @pl.when(core == 1)
     def _():
-        for kind, start, size in ((0, 0, most), (1, most, quarter)):
+        for span in (early, late):
+            add(0, span)
+        for start, size, kind in (early, late):
             at = pl.ds(start, size)
             inside, outside = close(start, size, kind)
             outside.wait_recv()
@@ -279,12 +276,12 @@
     out_ref[...] = jnp.dot(dia[...], rem[...], preferred_element_type=jnp.float32).astype(jnp.bfloat16)
 
     for s in range(pairs):
-        for copy in own(s) + relay(s) + (swap(s), onward(s)):
+        for copy in own(s) + relay(s) + tuple(f(s, span) for f in (swap, onward) for span in (early, late)):
             copy.wait_send()
     for p in range(PIECES):
         for copy in own_piece(p) + relay_piece(p):
             copy.wait_send()
-    for kind, start, size in ((0, 0, most), (1, most, quarter)):
+    for start, size, kind in (early, late):
         inside, outside = close(start, size, kind)
 
         @pl.when(core == 0)
@@ -306,7 +303,7 @@
     dma = pltpu.SemaphoreType.DMA
     return pl.pallas_call(
         functools.partial(kernel, n_col, n_rhs),
-        out_shape=jax.ShapeDtypeStruct((rows, cols), jnp.bfloat16),
+        out_shape=pltpu.VMEM((rows, cols), jnp.bfloat16),
         in_specs=[pl.BlockSpec(memory_space=pltpu.SMEM)] + [any_space] * 4,
         out_specs=pl.BlockSpec(memory_space=pltpu.VMEM),
         scratch_shapes=[
@@ -329,10 +326,10 @@
             dma((pairs, 4)),
             dma((PIECES, 4)),
             dma((PIECES, 4)),
-            dma((pairs,)),
-            dma((pairs,)),
-            dma((pairs,)),
-            dma((3, 2)),
+            dma((pairs, 2)),
+            dma((pairs, 2)),
+            dma((pairs, 2)),
+            dma((3, 2, 2)),
             dma((2,)),
             dma((2, 2)),
             pltpu.SemaphoreType.REGULAR,

time: 101 us -> 94.3 us (0.934)
  the two profiles are of different devices: /device:TPU:5 before, /device:TPU:1 now
where the time goes in v3:
time: 94.3 us; the launch traced here: 94.1 us
  Pallas kernels  93.3 us (99%)
    pallas_call x1, Pallas kernels, per_device(): pl.pallas_call(functools.partial(kernel, n_col, n_rhs), out_shape=pltpu.V...  93.3 us

profile of v3, /device:TPU:1, one launch (start us, length us, event | category | flops | bytes accessed | tf_op | source)
XLA Modules:
  0.0 94.1 jit_solution(7602891638151148971)
XLA Ops:
  0.0 93.3 %shard_map.55 = bf16[256,1024]{1,0:T(8,128)(2,1)S(1)} custom-call(s32[1,6]{1,0:T(1,128)} %tiles_ref.1, bf16[256,1024]{1,0:T(8,128)(2,1)} %rhs_hbm.1, bf16[3072,1024]{1,0:T(8,128)(2,1)} %sol_hbm.1, bf16[1,6,64,3072]{3,2,1,0:T(8,128)(2,1)} %fac_hbm.1, bf16[1,256,256]{2,1,0:T(8,128)(2,1)} %dia_hbm.1), custom_call_target="tpu_custom_call" | custom-call | tf_op jit(solution)/shard_map/pallas_call | solution.py:304
  93.3 0.8 copy.7

commit v4 on v3

--- a/solution.py
+++ b/solution.py
@@ -107,7 +107,7 @@
         lines = pl.ds(span[0], span[1])
         for target, which in ((give, 1 - core), (keep, core)):
 
-            @pl.loop(0, side // wide)
+            @pl.loop(0, side // wide, unroll=True)
             def _(block):
                 at = pl.multiple_of(which * side + block * wide, wide)
                 term = jnp.dot(fac[s, lines, :], sol[:, pl.ds(at, wide)], preferred_element_type=jnp.float32)
@@ -161,10 +161,8 @@
 
     def partial(p, span):
         lines, deep = pl.ds(span[0], span[1]), pl.ds(p * piece, piece)
-
-        @pl.loop(0, cols // wide)
-        def _(block):
-            at = pl.ds(pl.multiple_of(block * wide, wide), wide)
+        for block in range(2):
+            at = pl.ds(block * side, side)
             term = jnp.dot(fac[final, lines, deep], sol[deep, at], preferred_element_type=jnp.float32)
             if p > 0:
                 term = term + tail[lines, at]
@@ -209,18 +207,18 @@
                         copy.start()
 
         product(s, early)
-        combine(s, early)
         if s >= 1:
             for copy in relay(s - 1):
                 copy.wait_recv()
             product(s - 1, late)
+        combine(s, early)
+        if s >= 1:
             combine(s - 1, late)
     for span in (early, late):
         add(1, span, first=True)
     for copy in relay(end):
         copy.wait_recv()
     product(end, late)
-    combine(end, late)
 
     @pl.when(core == 0)
     def _():
@@ -228,19 +226,25 @@
         for p in range(PIECES):
             for copy in own_piece(p):
                 copy.start()
+        combine(end, late)
         for span in (early, late):
             add(2, span)
+        add(0, early)
+
+    @pl.when(core == 1)
+    def _():
+        pl.semaphore_signal(turn, inc=1, device_id=(partner, row), device_id_type=MESH)
 
     for p in range(PIECES):
-        if p == PIECES - 1:
-
-            @pl.when(core == 1)
-            def _():
-                pl.semaphore_signal(turn, inc=1, device_id=(partner, row), device_id_type=MESH)
-
         for copy, forward in zip(own_piece(p), relay_piece(p)):
             copy.wait_recv()
             forward.start()
+        if p == 1:
+
+            @pl.when(core == 1)
+            def _():
+                combine(end, late)
+
         partial(p, early)
     hand_over(*early)
     for p in range(PIECES):
@@ -249,30 +253,41 @@
         partial(p, late)
     hand_over(*late)
 
-    @pl.when(core == 0)
-    def _():
-        for span in (early, late):
-            add(0, span)
-
-    @pl.when(core == 1)
-    def _():
-        for span in (early, late):
-            add(0, span)
-        for start, size, kind in (early, late):
-            at = pl.ds(start, size)
-            inside, outside = close(start, size, kind)
-            outside.wait_recv()
-            for which in (0, 1):
-                there = pl.ds(which * side, side)
-                acc[at, there] = acc[at, there] + got[2, which, at, :].astype(jnp.float32)
-            inside.wait_recv()
-            acc[at, :] = acc[at, :] + near[at, :]
-
-    for slot, peer in enumerate((row, down, up, lax.rem(row + 2, n_rhs))):
+    def finish(span):
+        start, size, kind = span
+        at = pl.ds(start, size)
+        inside, outside = close(start, size, kind)
+        outside.wait_recv()
+        for which in (0, 1):
+            there = pl.ds(which * side, side)
+            acc[at, there] = acc[at, there] + got[2, which, at, :].astype(jnp.float32)
+        inside.wait_recv()
+        acc[at, :] = acc[at, :] + near[at, :]
+
+    def subtract(slot, peer):
         at = pl.ds(pl.multiple_of(peer * quarter, quarter), quarter)
         rem[at, :] = (
             rhs[at, :].astype(jnp.float32) - acc[pl.ds(slot * quarter, quarter), :]
         ).astype(jnp.bfloat16)
+
+    @pl.when(core == 1)
+    def _():
+        for span in (early, late):
+            add(0, span)
+        finish(early)
+
+    for slot, peer in enumerate((row, down, up)):
+        subtract(slot, peer)
+
+    @pl.when(core == 0)
+    def _():
+        add(0, late)
+
+    @pl.when(core == 1)
+    def _():
+        finish(late)
+
+    subtract(3, lax.rem(row + 2, n_rhs))
     out_ref[...] = jnp.dot(dia[...], rem[...], preferred_element_type=jnp.float32).astype(jnp.bfloat16)
 
     for s in range(pairs):

time: 94.3 us -> 91.4 us (0.969)
  Pallas kernels: 93.3 us -> 90.5 us
    pallas_call x1, Pallas kernels: 93.3 us -> 90.5 us  [per_device(): pl.pallas_call(functools.partial(kernel, n_col, n_rhs), out_shape=pltpu.V...]
where the time goes in v4:
time: 91.4 us; the launch traced here: 91.3 us
  Pallas kernels  90.5 us (99%)
    pallas_call x1, Pallas kernels, per_device(): pl.pallas_call(functools.partial(kernel, n_col, n_rhs), out_shape=pltpu.V...  90.5 us

profile of v4, /device:TPU:1, one launch (start us, length us, event | category | flops | bytes accessed | tf_op | source)
XLA Modules:
  0.0 91.3 jit_solution(4645150226287738061)
XLA Ops:
  0.0 90.5 %shard_map.55 = bf16[256,1024]{1,0:T(8,128)(2,1)S(1)} custom-call(s32[1,6]{1,0:T(1,128)} %tiles_ref.1, bf16[256,1024]{1,0:T(8,128)(2,1)} %rhs_hbm.1, bf16[3072,1024]{1,0:T(8,128)(2,1)} %sol_hbm.1, bf16[1,6,64,3072]{3,2,1,0:T(8,128)(2,1)} %fac_hbm.1, bf16[1,256,256]{2,1,0:T(8,128)(2,1)} %dia_hbm.1), custom_call_target="tpu_custom_call" | custom-call | tf_op jit(solution)/shard_map/pallas_call | solution.py:319
  90.5 0.8 copy.7

commit v5 on v4

--- a/solution.py
+++ b/solution.py
@@ -12,8 +12,8 @@
 PIECES = 4
 
 
-def kernel(n_col, n_rhs, tiles_ref, rhs_hbm, sol_hbm, fac_hbm, dia_hbm, out_ref,
-           sol, fac, rhs, dia, acc, rem, keep, give, take, part, got, tail, near, last,
+def kernel(n_col, n_rhs, tiles_hbm, rhs_hbm, sol_hbm, fac_hbm, dia_hbm, out_ref,
+           tiles_ref, sol, fac, rhs, dia, acc, rem, keep, give, take, part, got, tail, near, last,
            load_sem, y_send, y_recv, z_send, z_recv, c_send, c_recv, x_send, x_recv, t_send, t_recv, turn):
     hops, quarter = fac_hbm.shape[1], fac_hbm.shape[2]
     depth = fac_hbm.shape[3]
@@ -39,6 +39,7 @@
         pltpu.make_async_copy(sol_hbm, sol, load_sem.at[hops]),
         pltpu.make_async_copy(rhs_hbm, rhs, load_sem.at[hops + 1]),
         pltpu.make_async_copy(dia_hbm.at[0], dia, load_sem.at[hops + 2]),
+        pltpu.make_async_copy(tiles_hbm, tiles_ref, load_sem.at[hops + 3]),
     ]
 
     barrier = pltpu.get_barrier_semaphore()
@@ -64,7 +65,7 @@
         )
 
     def own(s):
-        src = fac_hbm.at[0, tile_of[s]]
+        src = fac_hbm.at[0, tile_of[s]] if s < 2 else fac.at[s, pl.ds(0, quarter), :]
         return (
             y_copy(src, s, quarter, quarter, 0, up),
             y_copy(src, s, 2 * quarter, quarter, 1, down),
@@ -85,7 +86,7 @@
         )
 
     def own_piece(p):
-        src = fac_hbm.at[0, tile_of[final]]
+        src = fac.at[final, pl.ds(0, quarter), :]
         return (
             z_copy(src, p, quarter, quarter, 0, up),
             z_copy(src, p, 2 * quarter, quarter, 1, down),
@@ -150,18 +151,23 @@
             term = got[slot, which, at, :].astype(jnp.float32)
             acc[at, there] = term if first else acc[at, there] + term
 
-    def close(start, size, kind):
-        at = pl.ds(start, size)
-        inside = remote(tail.at[at, :], near.at[at, :], t_send.at[kind], t_recv.at[0, kind], (partner, row))
+    def close(part_of):
+        start, size, kind = early if part_of == 0 else late
+        at, sides = pl.ds(start, size), (0, 1) if part_of == 0 else (part_of - 1,)
+        there = pl.ds(sides[0] * side, len(sides) * side)
+        which = pl.ds(sides[0], len(sides))
+        inside = remote(
+            tail.at[at, there], near.at[at, there], t_send.at[part_of], t_recv.at[0, part_of], (partner, row)
+        )
         outside = remote(
-            last.at[:, at, :], got.at[2, :, at, :], t_send.at[kind], t_recv.at[1, kind],
+            last.at[which, at, :], got.at[2, which, at, :], t_send.at[part_of], t_recv.at[1, part_of],
             (lax.rem(base + 7, n_col), row),
         )
-        return inside, outside
-
-    def partial(p, span):
+        return inside, outside, at, sides
+
+    def partial(p, span, blocks=(0, 1)):
         lines, deep = pl.ds(span[0], span[1]), pl.ds(p * piece, piece)
-        for block in range(2):
+        for block in blocks:
             at = pl.ds(block * side, side)
             term = jnp.dot(fac[final, lines, deep], sol[deep, at], preferred_element_type=jnp.float32)
             if p > 0:
@@ -170,8 +176,8 @@
                 term = term * weight(final)
             tail[lines, at] = term
 
-    def hand_over(start, size, kind):
-        inside, outside = close(start, size, kind)
+    def hand_over(part_of):
+        inside, outside, at, sides = close(part_of)
 
         @pl.when(core == 0)
         def _():
@@ -179,8 +185,7 @@
 
         @pl.when(core == 1)
         def _():
-            at = pl.ds(start, size)
-            for which in (0, 1):
+            for which in sides:
                 last[which, at, :] = tail[at, pl.ds(which * side, side)].astype(jnp.bfloat16)
             outside.start()
 
@@ -246,49 +251,57 @@
                 combine(end, late)
 
         partial(p, early)
-    hand_over(*early)
+    hand_over(0)
     for p in range(PIECES):
         for copy in relay_piece(p):
             copy.wait_recv()
-        partial(p, late)
-    hand_over(*late)
-
-    def finish(span):
-        start, size, kind = span
-        at = pl.ds(start, size)
-        inside, outside = close(start, size, kind)
+        if p < PIECES - 1:
+            partial(p, late)
+    for which in (0, 1):
+        partial(PIECES - 1, late, (which,))
+        hand_over(which + 1)
+
+    def finish(part_of):
+        inside, outside, at, sides = close(part_of)
         outside.wait_recv()
-        for which in (0, 1):
+        for which in sides:
             there = pl.ds(which * side, side)
             acc[at, there] = acc[at, there] + got[2, which, at, :].astype(jnp.float32)
         inside.wait_recv()
-        acc[at, :] = acc[at, :] + near[at, :]
-
-    def subtract(slot, peer):
+        for which in sides:
+            there = pl.ds(which * side, side)
+            acc[at, there] = acc[at, there] + near[at, there]
+
+    def subtract(slot, peer, there):
         at = pl.ds(pl.multiple_of(peer * quarter, quarter), quarter)
-        rem[at, :] = (
-            rhs[at, :].astype(jnp.float32) - acc[pl.ds(slot * quarter, quarter), :]
+        rem[at, there] = (
+            rhs[at, there].astype(jnp.float32) - acc[pl.ds(slot * quarter, quarter), there]
         ).astype(jnp.bfloat16)
 
     @pl.when(core == 1)
     def _():
         for span in (early, late):
             add(0, span)
-        finish(early)
+        finish(0)
 
     for slot, peer in enumerate((row, down, up)):
-        subtract(slot, peer)
+        subtract(slot, peer, pl.ds(0, cols))
 
     @pl.when(core == 0)
     def _():
         add(0, late)
 
-    @pl.when(core == 1)
-    def _():
-        finish(late)
-
-    subtract(3, lax.rem(row + 2, n_rhs))
-    out_ref[...] = jnp.dot(dia[...], rem[...], preferred_element_type=jnp.float32).astype(jnp.bfloat16)
+    for which in (0, 1):
+        there = pl.ds(which * side, side)
+
+        @pl.when(core == 1)
+        def _():
+            finish(which + 1)
+
+        subtract(3, lax.rem(row + 2, n_rhs), there)
+        out_ref[:, there] = jnp.dot(
+            dia[...], rem[:, there], preferred_element_type=jnp.float32
+        ).astype(jnp.bfloat16)
 
     for s in range(pairs):
         for copy in own(s) + relay(s) + tuple(f(s, span) for f in (swap, onward) for span in (early, late)):
@@ -296,8 +309,8 @@
     for p in range(PIECES):
         for copy in own_piece(p) + relay_piece(p):
             copy.wait_send()
-    for start, size, kind in (early, late):
-        inside, outside = close(start, size, kind)
+    for part_of in range(3):
+        inside, outside, _, _ = close(part_of)
 
         @pl.when(core == 0)
         def _():
@@ -319,9 +332,10 @@
     return pl.pallas_call(
         functools.partial(kernel, n_col, n_rhs),
         out_shape=pltpu.VMEM((rows, cols), jnp.bfloat16),
-        in_specs=[pl.BlockSpec(memory_space=pltpu.SMEM)] + [any_space] * 4,
+        in_specs=[any_space] * 5,
         out_specs=pl.BlockSpec(memory_space=pltpu.VMEM),
         scratch_shapes=[
+            pltpu.SMEM((1, hops), jnp.int32),
             pltpu.VMEM((depth, cols), jnp.bfloat16),
             pltpu.VMEM((hops, rows, depth), jnp.bfloat16),
             pltpu.VMEM((rows, cols), jnp.bfloat16),
@@ -336,7 +350,7 @@
             pltpu.VMEM((rows, cols), jnp.float32),
             pltpu.VMEM((rows, cols), jnp.float32),
             pltpu.VMEM((2, rows, side), jnp.bfloat16),
-            dma((hops + 3,)),
+            dma((hops + 4,)),
             dma((pairs, 4)),
             dma((pairs, 4)),
             dma((PIECES, 4)),
@@ -345,8 +359,8 @@
             dma((pairs, 2)),
             dma((pairs, 2)),
             dma((3, 2, 2)),
-            dma((2,)),
-            dma((2, 2)),
+            dma((3,)),
+            dma((2, 3)),
             pltpu.SemaphoreType.REGULAR,
         ],
         compiler_params=pltpu.CompilerParams(

time: 91.4 us -> 90.6 us (level)
  no operation moved by 1% of the time
where the time goes in v5:
time: 90.6 us; the launch traced here: 90.5 us
  Pallas kernels  89.7 us (99%)
    pallas_call x1, Pallas kernels, per_device(): pl.pallas_call(functools.partial(kernel, n_col, n_rhs), out_shape=pltpu.V...  89.7 us

profile of v5, /device:TPU:1, one launch (start us, length us, event | category | flops | bytes accessed | tf_op | source)
XLA Modules:
  0.0 90.5 jit_solution(5831873784206746931)
XLA Ops:
  0.0 89.7 %shard_map.55 = bf16[256,1024]{1,0:T(8,128)(2,1)S(1)} custom-call(s32[1,6]{1,0:T(1,128)} %tiles_hbm.1, bf16[256,1024]{1,0:T(8,128)(2,1)} %rhs_hbm.1, bf16[3072,1024]{1,0:T(8,128)(2,1)} %sol_hbm.1, bf16[1,6,64,3072]{3,2,1,0:T(8,128)(2,1)} %fac_hbm.1, bf16[1,256,256]{2,1,0:T(8,128)(2,1)} %dia_hbm.1), custom_call_target="tpu_custom_call" | custom-call | tf_op jit(solution)/shard_map/pallas_call | solution.py:332
  89.7 0.8 copy.7
